TPU v7x, 32 devices: a whole 2x2x4 slice. The times are simulated.
32 devices in a mesh: member: 2 (over y), lon: 4 (over z), lat: 2 (over x), dp: 2 (over core).
Axes of the slice: x: 2, y: 2, z: 4, core: 2. Of those that a mesh axis runs over, the one named last changes fastest.
Arguments:
- fields: bfloat16 [4, 64, 32, 512], P(('member', 'dp'), 'lat', 'lon'), parts along dimension 0, may hold values from -6 to 6
- cotangent: bfloat16 [4, 64, 32, 512], P(('member', 'dp'), 'lat', 'lon'), parts along dimension 0, may hold values from -6 to 6
- conv_weight: float32 [7, 7, 512], replicated, may hold values from -0.875 to 0.875
- norm_gain: float32 [512], replicated, may hold values from 0.1 to 1.9
- w_qkv: bfloat16 [512, 768], replicated, may hold values from -1 to 1
- w_out: bfloat16 [256, 512], replicated, may hold values from -0.375 to 0.375
Outputs:
- result: bfloat16 [4, 64, 32, 512], P(('member', 'dp'), 'lat', 'lon'), parts along dimension 0
- grad_fields: bfloat16 [4, 64, 32, 512], P(('member', 'dp'), 'lat', 'lon'), parts along dimension 0
- grad_qkv: float32 [1024, 768], P('member'), parts along dimension 0
- grad_out: float32 [512, 512], P('member'), parts along dimension 0
- grad_conv: float32 [14, 7, 512], P('member'), parts along dimension 0
- grad_gain: float32 [1024], P('member'), parts along dimension 0
There are 2 independent parts, one for each index of `member`. A program takes and returns all parts, laid end to end along the dimension named above; an argument that names none is the same for every part. Nothing has to cross between parts.
All inputs are finite; a program needn't handle non-finite values.
Results may differ from a plain program's by a relative error of at most 0.012.
The roundings to bfloat16 on the way count: a program that leaves them out, or rounds other values in their place, can miss the bound.
Values may be sent and summed in bfloat16 or wider, within the bound.
A program may use at most 64 MiB of HBM per device.

v0:
```python
import functools
import itertools

import jax
import jax.numpy as jnp
from jax import lax
from jax.experimental import pallas as pl
from jax.experimental.pallas import tpu as pltpu
from jax.sharding import PartitionSpec as P

HEADS = 4
HEAD_DIM = 64


EPSILON = 1e-06


def with_halo(x, sides, width, wrap):
    for axis, dim in sides:
        size, length = (lax.axis_size(axis), x.shape[dim])
        up = [(i, (i + 1) % size) for i in range(size if wrap else size - 1)]
        down = [(j, i) for i, j in up]
        last = lax.slice_in_dim(x, length - width, length, axis=dim)
        first = lax.slice_in_dim(x, 0, width, axis=dim)
        before = lax.ppermute(last, axis, up)
        after = lax.ppermute(first, axis, down)
        x = jnp.concatenate([before, x, after], axis=dim)
    return x


def spread(padded, kernel, lat_rows, lon_cols):
    summed = jnp.zeros(padded.shape[:1] + (lat_rows, lon_cols, padded.shape[3]), jnp.float32)
    for row_shift in range(7):
        band = padded[:, row_shift : row_shift + lat_rows].astype(jnp.float32)
        partial_row = kernel[row_shift, 0] * band[:, :, 0:lon_cols]
        for col_shift in range(1, 7):
            partial_row = (
                partial_row
                + kernel[row_shift, col_shift] * band[:, :, col_shift : col_shift + lon_cols]
            )
        summed = summed + partial_row
    return summed


def correlate(padded, upstream, lat_rows, lon_cols):
    pieces = []
    for row_shift in range(7):
        for col_shift in range(7):
            window = padded[
                :, row_shift : row_shift + lat_rows, col_shift : col_shift + lon_cols
            ].astype(jnp.float32)
            pieces.append(jnp.sum(window * upstream, axis=(0, 1, 2)))
    return jnp.stack(pieces).reshape(7, 7, -1)


def split_heads(values):
    return values.reshape(values.shape[:-1] + (HEADS, HEAD_DIM))


def attend_forward(rowwise, att_width):
    queries = split_heads(rowwise[..., :att_width])
    keys_part = split_heads(rowwise[..., att_width : 2 * att_width])
    values_part = split_heads(rowwise[..., 2 * att_width :])
    scores = jnp.einsum(
        "brqhd,brkhd->brhqk", queries, keys_part, preferred_element_type=jnp.float32
    ) * HEAD_DIM ** (-0.5)
    row_peak = jnp.max(scores, -1, keepdims=True)
    raised = jnp.exp(scores - row_peak)
    probs = raised / jnp.sum(raised, -1, keepdims=True)
    weights = probs.astype(jnp.bfloat16)
    mixed = jnp.einsum(
        "brhqk,brkhd->brqhd", weights, values_part, preferred_element_type=jnp.float32
    )
    return (mixed.reshape(rowwise.shape[:3] + (att_width,)).astype(jnp.bfloat16), probs)


def attend_backward(rowwise, probs, grad_rowwise, att_width):
    queries = split_heads(rowwise[..., :att_width])
    keys_part = split_heads(rowwise[..., att_width : 2 * att_width])
    values_part = split_heads(rowwise[..., 2 * att_width :])
    grad_heads = split_heads(grad_rowwise)
    weights = probs.astype(jnp.bfloat16)
    grad_probs = jnp.einsum(
        "brqhd,brkhd->brhqk", grad_heads, values_part, preferred_element_type=jnp.float32
    )
    inner = jnp.sum(probs * grad_probs, -1, keepdims=True)
    grad_scores = (probs * (grad_probs - inner) * HEAD_DIM ** (-0.5)).astype(jnp.bfloat16)
    grad_query = jnp.einsum(
        "brhqk,brkhd->brqhd", grad_scores, keys_part, preferred_element_type=jnp.float32
    )
    grad_key = jnp.einsum(
        "brhqk,brqhd->brkhd", grad_scores, queries, preferred_element_type=jnp.float32
    )
    grad_value = jnp.einsum(
        "brhqk,brqhd->brkhd", weights, grad_heads, preferred_element_type=jnp.float32
    )
    shaped = rowwise.shape[:3] + (att_width,)
    return jnp.concatenate(
        [
            grad_query.reshape(shaped).astype(jnp.bfloat16),
            grad_key.reshape(shaped).astype(jnp.bfloat16),
            grad_value.reshape(shaped).astype(jnp.bfloat16),
        ],
        axis=-1,
    )


def contract_rows(left, right):
    return lax.dot_general(
        left, right, (((0,), (0,)), ((), ())), preferred_element_type=jnp.float32
    )


def contract_cols(left, right):
    return lax.dot_general(
        left, right, (((1,), (1,)), ((), ())), preferred_element_type=jnp.float32
    )


def on_device_native(fields, cotangent, conv_weight, norm_gain, w_qkv, w_out):
    batch_count, lat_rows, lon_cols, channels = fields.shape
    att_width = w_out.shape[0]
    wide = with_halo(fields, (("lon", 2),), 3, True)
    padded = with_halo(wide, (("lat", 1),), 3, False)
    update = fields.astype(jnp.float32) + spread(padded, conv_weight, lat_rows, lon_cols)
    inverse = lax.rsqrt(jnp.mean(update * update, -1, keepdims=True) + EPSILON)
    normed = (update * inverse * norm_gain).astype(jnp.bfloat16)
    normed_flat = normed.reshape(-1, channels)
    projected = jnp.dot(normed_flat, w_qkv, preferred_element_type=jnp.float32).astype(jnp.bfloat16)
    rowwise = lax.all_to_all(
        projected.reshape(batch_count, lat_rows, lon_cols, 3 * att_width),
        "lon",
        split_axis=1,
        concat_axis=2,
        tiled=True,
    )
    mixed_rows, probs = attend_forward(rowwise, att_width)
    mixed = lax.all_to_all(mixed_rows, "lon", split_axis=2, concat_axis=1, tiled=True)
    mixed_flat = mixed.reshape(-1, att_width)
    result = (
        update
        + jnp.dot(mixed_flat, w_out, preferred_element_type=jnp.float32).reshape(update.shape)
    ).astype(jnp.bfloat16)
    upstream_flat = cotangent.reshape(-1, channels)
    grad_mixed = contract_cols(upstream_flat, w_out).astype(jnp.bfloat16)
    grad_out = contract_rows(mixed_flat, upstream_flat)
    grad_rowwise = lax.all_to_all(
        grad_mixed.reshape(batch_count, lat_rows, lon_cols, att_width),
        "lon",
        split_axis=1,
        concat_axis=2,
        tiled=True,
    )
    grad_projected_rows = attend_backward(rowwise, probs, grad_rowwise, att_width)
    grad_projected = lax.all_to_all(
        grad_projected_rows, "lon", split_axis=2, concat_axis=1, tiled=True
    )
    grad_flat = grad_projected.reshape(-1, 3 * att_width)
    grad_weight = contract_rows(normed_flat, grad_flat)
    grad_normed = contract_cols(grad_flat, w_qkv).reshape(update.shape)
    grad_gain = jnp.sum(grad_normed * (update * inverse), axis=(0, 1, 2))
    gained = norm_gain * grad_normed
    grad_update = (
        cotangent.astype(jnp.float32)
        + inverse * gained
        - update * inverse**3 * jnp.mean(gained * update, -1, keepdims=True)
    )
    grad_wide = with_halo(grad_update.astype(jnp.bfloat16), (("lon", 2),), 3, True).astype(
        grad_update.dtype
    )
    grad_padded = with_halo(grad_wide.astype(jnp.bfloat16), (("lat", 1),), 3, False).astype(
        grad_wide.dtype
    )
    grad_fields = (
        grad_update + spread(grad_padded, conv_weight[::-1, ::-1], lat_rows, lon_cols)
    ).astype(jnp.bfloat16)
    grad_conv = correlate(padded, grad_update, lat_rows, lon_cols)
    totals = lax.psum((grad_weight, grad_out, grad_conv, grad_gain), ("lon", "lat", "dp"))
    return (result, grad_fields, totals[0], totals[1], totals[2], totals[3])


MESH = pl.DeviceIdType.MESH
AXES = ("lat", "lon", "dp")
LANES = 128


def place():
    return tuple(lax.axis_index(a) for a in AXES)


def greet(sizes):
    me = place()
    barrier = pltpu.get_barrier_semaphore()
    count = 0
    for offset in itertools.product(*(range(s) for s in sizes)):
        if not any(offset):
            continue
        target = {a: lax.rem(m + o, s) for a, m, o, s in zip(AXES, me, offset, sizes)}
        pl.semaphore_signal(barrier, inc=1, device_id=target, device_id_type=MESH)
        count += 1
    pl.semaphore_wait(barrier, count)


def remote(src, dst, send, recv, target):
    return pltpu.make_async_remote_copy(
        src_ref=src, dst_ref=dst, send_sem=send, recv_sem=recv, device_id=target, device_id_type=MESH
    )


def bring_rows(sizes, f_ref, c_ref, fp_ref, cr_ref, send, recv, xsend, xrecv, local):
    n_lat, n_lon, _ = sizes
    lat, lon, _ = place()
    rows = f_ref.shape[0]
    own = rows // n_lon

    def span(j):
        low, high = max(0, own * j - 3), min(rows, own * j + own + 3)
        start = low - (own * j - 3)
        return slice(low, high), slice(start, start + high - low)

    def fields_copy(i, j):
        there, here = span(j)
        return remote(f_ref.at[there], fp_ref.at[here, i], send.at[0, j], recv.at[0, i], {"lon": j})

    def cot_copy(i, j):
        return remote(
            c_ref.at[own * j : own * j + own], cr_ref.at[:, i], send.at[1, j], recv.at[1, i], {"lon": j}
        )

    def fields_own(j):
        there, here = span(j)
        return pltpu.make_async_copy(f_ref.at[there], fp_ref.at[here, j], local.at[0])

    def cot_own(j):
        return pltpu.make_async_copy(c_ref.at[own * j : own * j + own], cr_ref.at[:, j], local.at[1])

    def below(i):
        return remote(
            f_ref.at[rows - 3 : rows], fp_ref.at[0:3, i], xsend.at[0], xrecv.at[0, i],
            {"lat": lat + 1, "lon": 0},
        )

    def above(i):
        return remote(
            f_ref.at[0:3], fp_ref.at[own + 3 : own + 6, i], xsend.at[1], xrecv.at[1, i],
            {"lat": lat - 1, "lon": n_lon - 1},
        )

    def start():
        for j in range(n_lon):

            @pl.when(lon != j)
            def _(j=j):
                fields_copy(lon, j).start()

        @pl.when(lat < n_lat - 1)
        def _():
            below(lon).start()

        @pl.when(lat > 0)
        def _():
            above(lon).start()

        for j in range(n_lon):

            @pl.when(lon != j)
            def _(j=j):
                cot_copy(lon, j).start()

            @pl.when(lon == j)
            def _(j=j):
                fields_own(j).start()
                cot_own(j).start()

        @pl.when((lat == 0) & (lon == 0))
        def _():
            fp_ref[0:3] = jnp.zeros((3,) + fp_ref.shape[1:], fp_ref.dtype)

        @pl.when((lat == n_lat - 1) & (lon == n_lon - 1))
        def _():
            fp_ref[own + 3 : own + 6] = jnp.zeros((3,) + fp_ref.shape[1:], fp_ref.dtype)

    def wait_fields():
        for j in range(n_lon):

            @pl.when(lon == j)
            def _(j=j):
                fields_own(j).wait()
                for i in range(n_lon):
                    if i != j:
                        fields_copy(i, j).wait_recv()

        @pl.when((lat > 0) & (lon == 0))
        def _():
            for i in range(n_lon):
                below(i).wait_recv()

        @pl.when((lat < n_lat - 1) & (lon == n_lon - 1))
        def _():
            for i in range(n_lon):
                above(i).wait_recv()

    def wait_cot():
        for j in range(n_lon):

            @pl.when(lon == j)
            def _(j=j):
                cot_own(j).wait()
                for i in range(n_lon):
                    if i != j:
                        cot_copy(i, j).wait_recv()

    def wait_sent():
        for j in range(n_lon):

            @pl.when(lon != j)
            def _(j=j):
                fields_copy(lon, j).wait_send()
                cot_copy(lon, j).wait_send()

        @pl.when(lat < n_lat - 1)
        def _():
            below(lon).wait_send()

        @pl.when(lat > 0)
        def _():
            above(lon).wait_send()

    return start, wait_fields, wait_cot, wait_sent


def convolve(pad, weight, out, own, flip):
    circle, channels = pad.shape[1], pad.shape[2]
    for c in range(channels // LANES):
        lanes = slice(c * LANES, (c + 1) * LANES)

        def row(r, carry, lanes=lanes):
            bands = [pad[r + a, :, lanes] for a in range(7)]
            total = bands[3]
            for e in range(7):
                part = None
                for a in range(7):
                    tap = weight[6 - a if flip else a, (6 - e if flip else e) : (7 - e if flip else e + 1), lanes]
                    term = bands[a] * tap
                    part = term if part is None else part + term
                turn = (3 - e) % circle
                if turn:
                    part = pltpu.roll(part, turn, 0)
                total = total + part
            out[r, :, lanes] = total
            return carry

        lax.fori_loop(0, own, row, 0)


def correlate_rows(pad, upstream, out, own):
    circle, channels = pad.shape[1], pad.shape[2]

    def chunk(c, carry):
        lanes = pl.ds(pl.multiple_of(c * LANES, LANES), LANES)
        for e in range(7):
            turn = (e - 3) % circle
            turned = [upstream[r, :, lanes] for r in range(own)]
            if turn:
                turned = [pltpu.roll(t, turn, 0) for t in turned]
            for a in range(7):
                total = None
                for r in range(own):
                    term = pad[r + a, :, lanes] * turned[r]
                    total = term if total is None else total + term
                out[a, e : e + 1, lanes] = jnp.sum(total, axis=0, keepdims=True)
        return carry

    lax.fori_loop(0, channels // LANES, chunk, 0)


def dot(left, right, dims):
    return lax.dot_general(left, right, (dims, ((), ())), preferred_element_type=jnp.float32)


PLAIN, COLS, ROWS = ((1,), (0,)), ((1,), (1,)), ((0,), (0,))


def attend_rows(projected, circle, att_width):
    cells = projected.shape[0]
    group = max(circle, LANES)
    row_of = lax.broadcasted_iota(jnp.int32, (group, group), 0) // circle
    col_of = lax.broadcasted_iota(jnp.int32, (group, group), 1) // circle
    same = row_of == col_of
    lane_head = lax.broadcasted_iota(jnp.int32, (group, LANES), 1) // HEAD_DIM
    bf16 = jnp.bfloat16
    zero = jnp.zeros((), bf16)
    heads = range(LANES // HEAD_DIM)
    groups = [slice(g * group, (g + 1) * group) for g in range(cells // group)]
    pairs = [slice(p * LANES, (p + 1) * LANES) for p in range(att_width // LANES)]

    def third(k, cut, at):
        return projected[cut, k * att_width : (k + 1) * att_width][:, at]

    def join(parts):
        whole = parts[0]
        for h in heads[1:]:
            whole = jnp.where(lane_head == h, parts[h], whole)
        return whole.astype(bf16)

    kept, mixed = {}, []
    for g, cut in enumerate(groups):
        found = []
        for p, at in enumerate(pairs):
            q, k, v = (third(n, cut, at) for n in range(3))
            parts = []
            for h in heads:
                scores = dot(jnp.where(lane_head == h, q, zero), k, COLS) * HEAD_DIM ** (-0.5)
                scores = jnp.where(same, scores, -jnp.inf)
                raised = jnp.exp(scores - jnp.max(scores, -1, keepdims=True))
                probs = raised / jnp.sum(raised, -1, keepdims=True)
                kept[g, p, h] = probs
                parts.append(dot(probs.astype(bf16), v, PLAIN))
            found.append(join(parts))
        mixed.append(jnp.concatenate(found, axis=1))

    def backward(grad_mixed):
        grads = []
        for g, cut in enumerate(groups):
            found = [[], [], []]
            for p, at in enumerate(pairs):
                q, k, v = (third(n, cut, at) for n in range(3))
                up = grad_mixed[cut, at]
                parts = [[], [], []]
                for h in heads:
                    probs = kept[g, p, h]
                    grad_probs = dot(jnp.where(lane_head == h, up, zero), v, COLS)
                    inner = jnp.sum(probs * grad_probs, -1, keepdims=True)
                    grad_scores = (probs * (grad_probs - inner) * HEAD_DIM ** (-0.5)).astype(bf16)
                    parts[0].append(dot(grad_scores, k, PLAIN))
                    parts[1].append(dot(grad_scores, q, ROWS))
                    parts[2].append(dot(probs.astype(bf16), up, ROWS))
                for part, into in zip(parts, found):
                    into.append(join(part))
            grads.append(jnp.concatenate(found[0] + found[1] + found[2], axis=1))
        return jnp.concatenate(grads, axis=0)

    return jnp.concatenate(mixed, axis=0), backward


def core_step(cr_ref, update_ref, gain, wq_ref, wo_ref, result_ref, gu_ref, gub_ref, big1_ref, big3_ref, go_ref, gg_ref):
    own, blocks, width, channels = cr_ref.shape
    circle, cells = blocks * width, own * blocks * width
    att_width = wo_ref.shape[0]
    update = update_ref[...].reshape(cells, channels)
    inverse = lax.rsqrt(jnp.mean(update * update, -1, keepdims=True) + EPSILON)
    normed = (update * inverse * gain).astype(jnp.bfloat16)
    projected = dot(normed, wq_ref[...], PLAIN).astype(jnp.bfloat16)
    mixed, backward = attend_rows(projected, circle, att_width)
    result = update + dot(mixed, wo_ref[...], PLAIN)
    result_ref[...] = result.reshape(result_ref.shape).astype(jnp.bfloat16)
    yield
    cot32 = cr_ref[...].astype(jnp.float32).reshape(cells, channels)
    cot = cot32.astype(jnp.bfloat16)
    grad_mixed = dot(cot, wo_ref[...], COLS).astype(jnp.bfloat16)
    grad_projected = backward(grad_mixed)
    grad_normed = dot(grad_projected, wq_ref[...], COLS)
    gained = gain * grad_normed
    grad_update = (
        cot32
        + inverse * gained
        - update * (inverse * inverse * inverse) * jnp.mean(gained * update, -1, keepdims=True)
    )
    gu_ref[...] = grad_update.reshape(gu_ref.shape)
    gub_ref[...] = grad_update.reshape(gub_ref.shape).astype(jnp.bfloat16)
    yield
    grad_weight = dot(normed, grad_projected, ROWS).astype(jnp.bfloat16)
    half = big1_ref.shape[2]
    big1_ref[...] = grad_weight[:, :half].reshape(big1_ref.shape)
    big3_ref[...] = grad_weight[:, half:].reshape(big3_ref.shape)
    yield
    gg_ref[...] = jnp.sum(grad_normed * (update * inverse), axis=0, keepdims=True)
    go_ref[...] = dot(mixed, cot, ROWS)
    yield


def halo_rows(sizes, g_ref, top_ref, low_ref, send, recv):
    n_lat, n_lon, _ = sizes
    lat, lon, _ = place()
    own = g_ref.shape[0]
    index, last = lat * n_lon + lon, n_lat * n_lon - 1

    def at(k):
        k = lax.rem(k + n_lat * n_lon, n_lat * n_lon)
        return {"lat": k // n_lon, "lon": lax.rem(k, n_lon)}

    down = remote(g_ref.at[own - 3 : own], top_ref, send.at[0], recv.at[0], at(index + 1))
    up = remote(g_ref.at[0:3], low_ref, send.at[1], recv.at[1], at(index - 1))

    def start():
        @pl.when(index < last)
        def _():
            down.start()

        @pl.when(index > 0)
        def _():
            up.start()

        @pl.when(index == 0)
        def _():
            top_ref[...] = jnp.zeros_like(top_ref)

        @pl.when(index == last)
        def _():
            low_ref[...] = jnp.zeros_like(low_ref)

    def wait():
        @pl.when(index > 0)
        def _():
            down.wait_recv()
            up.wait_send()

        @pl.when(index < last)
        def _():
            up.wait_recv()
            down.wait_send()

    return start, wait


def pack(big, go_ref, conv, gg_ref):
    parts, rows, _ = big.shape
    att, channels = go_ref.shape
    bf16 = jnp.bfloat16
    fold = parts * rows // att
    part = channels // fold
    for k in range(fold):
        piece = go_ref[:, k * part : (k + 1) * part].astype(bf16).reshape(parts // fold, rows, part)
        big[k * (parts // fold) : (k + 1) * (parts // fold), :, :part] = piece
    small = jnp.concatenate(
        [conv[a] for a in range(7)] + [gg_ref[...], jnp.zeros((64 - 50, channels), jnp.float32)], axis=0
    )
    step = 64 // rows
    used = channels // LANES * step
    for k in range(channels // LANES):
        piece = small[:, k * LANES : (k + 1) * LANES].astype(bf16).reshape(step, rows, LANES)
        big[k * step : (k + 1) * step, :, part:] = piece
    if used < parts:
        big[used:, :, part:] = jnp.zeros((parts - used, rows, LANES), bf16)


def finish(one_ref, three_ref, two_ref, result_ref, gf_ref, result_out, gf_out, gq_out, go_out, gc_out, gg_out):
    parts, rows, _ = two_ref.shape
    att, channels = go_out.shape
    fold = parts * rows // att
    part = channels // fold
    f32 = jnp.float32
    result_out[...] = result_ref[...]
    gf_out[...] = gf_ref[...]
    half = one_ref.shape[2]
    gq_out[:, :half] = one_ref[...].astype(f32).reshape(parts * rows, half)
    gq_out[:, half:] = three_ref[...].astype(f32).reshape(parts * rows, half)
    for k in range(fold):
        piece = two_ref[k * (parts // fold) : (k + 1) * (parts // fold), :, :part]
        go_out[:, k * part : (k + 1) * part] = piece.astype(f32).reshape(att, part)
    step = 64 // rows
    for k in range(channels // LANES):
        lanes = slice(k * LANES, (k + 1) * LANES)
        small = two_ref[k * step : (k + 1) * step, :, part:].astype(f32).reshape(64, LANES)
        for a in range(7):
            gc_out[a, :, lanes] = small[a * 7 : (a + 1) * 7]
        gg_out[:, lanes] = small[49:50]


def give_rows(n_lon, lon, src, dst, send, recv):
    own = src.shape[0]

    def copy(i, j):
        return remote(src.at[:, j], dst.at[pl.ds(i * own, own)], send.at[j], recv.at[i], {"lon": j})

    def start():
        for j in range(n_lon):

            @pl.when(lon != j)
            def _(j=j):
                copy(lon, j).start()

            @pl.when(lon == j)
            def _(j=j):
                dst[j * own : (j + 1) * own] = src[:, j]

    def wait():
        for j in range(n_lon):

            @pl.when(lon == j)
            def _(j=j):
                for i in range(n_lon):
                    if i != j:
                        copy(i, j).wait_recv()

            @pl.when(lon != j)
            def _(j=j):
                copy(lon, j).wait_send()

    return start, wait


def sum_stages(sizes, big, all_ref, got1, sum1, got2, sum2, got3, send, recv):
    n_lat, n_lon, n_dp = sizes
    lat, lon, dp = place()
    half, quarter = n_lat * n_lon, n_lon
    f32 = jnp.float32
    other_dp, other_lat = 1 - dp, 1 - lat
    mine = dp * half + lat * quarter
    one = remote(big.at[pl.ds(other_dp * half, half)], got1, send.at[0], recv.at[0], {"dp": other_dp})
    two = remote(sum1.at[pl.ds(other_lat * quarter, quarter)], got2, send.at[1], recv.at[1], {"lat": other_lat})

    def three(i, j):
        return remote(sum2.at[j], got3.at[i], send.at[2 + j], recv.at[2 + i], {"lon": j})

    base = 2 + n_lon

    def four(i, j):
        spot = all_ref.at[mine + i]
        return remote(spot, spot, send.at[base + j], recv.at[base + i], {"lon": j})

    base2 = base + n_lon

    def five(side):
        spot = all_ref.at[pl.ds(dp * half + side * quarter, quarter)]
        return remote(spot, spot, send.at[base2], recv.at[base2], {"lat": other_lat})

    def six(side):
        spot = all_ref.at[pl.ds(side * half, half)]
        return remote(spot, spot, send.at[base2 + 1], recv.at[base2 + 1], {"dp": other_dp})

    def others(do):
        for j in range(n_lon):

            @pl.when(lon != j)
            def _(j=j):
                do(j)

    def s0():
        one.start()

    def s1():
        one.wait()
        for k in range(half):
            sum1[k] = (big[dp * half + k].astype(f32) + got1[k].astype(f32)).astype(sum1.dtype)
        two.start()

    def s2():
        two.wait()
        for k in range(quarter):
            sum2[k] = (sum1[lat * quarter + k].astype(f32) + got2[k].astype(f32)).astype(sum2.dtype)
        others(lambda j: three(lon, j).start())
        got3[lon] = sum2[lon]

    def s3():
        others(lambda j: three(j, j).wait_recv())
        others(lambda j: three(lon, j).wait_send())
        total = got3[0].astype(f32)
        for i in range(1, n_lon):
            total = total + got3[i].astype(f32)
        all_ref[mine + lon] = total.astype(all_ref.dtype)
        others(lambda j: four(lon, j).start())

    def s4():
        others(lambda j: four(j, j).wait_recv())
        others(lambda j: four(lon, j).wait_send())
        five(lat).start()

    def s5():
        five(lat).wait_send()
        five(other_lat).wait_recv()
        six(dp).start()

    def s6():
        six(dp).wait_send()
        six(other_dp).wait_recv()

    return s0, s1, s2, s3, s4, s5, s6


def layer(sizes, f_ref, c_ref, w_hbm, gain_ref, wq_hbm, wo_hbm,
          result_out, gf_out, every1, every3, every2,
          fp, cr, weight, wq, wo, pad, update, result, gu, gub, go, gg, top, low, gpad, out, gf, conv,
          big1, a1, b1, c1, d1, e1, big3, a3, b3, c3, d3, e3, big2, a2, b2, c2, d2, e2,
          send, recv, xsend, xrecv, local, hsend, hrecv, rsend, rrecv, gsend, grecv, s1, r1, s3, r3, s2, r2):
    n_lat, n_lon, _ = sizes
    lat, lon, dp = place()
    own, circle, channels = gu.shape
    f32, bf16 = jnp.float32, jnp.bfloat16
    loads = [
        pltpu.make_async_copy(src, dst, local.at[2 + k])
        for k, (src, dst) in enumerate(((w_hbm, weight), (wq_hbm, wq), (wo_hbm, wo)))
    ]
    for load in loads:
        load.start()
    one = sum_stages(sizes, big1, every1, a1, b1, c1, d1, e1, s1, r1)
    three = sum_stages(sizes, big3, every3, a3, b3, c3, d3, e3, s3, r3)
    two = sum_stages(sizes, big2, every2, a2, b2, c2, d2, e2, s2, r2)
    start_in, wait_fields, wait_cot, wait_sent = bring_rows(
        sizes, f_ref, c_ref, fp, cr, send, recv, xsend, xrecv, local
    )
    start_h, wait_h = halo_rows(sizes, gub, top, low, hsend, hrecv)
    start_r, wait_r = give_rows(n_lon, lon, result, result_out, rsend, rrecv)
    start_g, wait_g = give_rows(n_lon, lon, gf, gf_out, gsend, grecv)
    greet(sizes)
    start_in()
    loads[0].wait()
    wait_fields()
    pad[...] = fp[...].astype(f32).reshape(pad.shape)
    convolve(pad, weight, update, own, False)
    for load in loads[1:]:
        load.wait()
    steps = core_step(cr, update, gain_ref[...], wq, wo, result, gu, gub, big1, big3, go, gg)
    next(steps)
    start_r()
    wait_cot()
    next(steps)
    start_h()
    next(steps)
    one[0]()
    three[0]()
    next(steps)
    correlate_rows(pad, gu, conv, own)
    pack(big2, go, conv, gg)
    two[0]()
    one[1]()
    three[1]()
    wait_h()
    gpad[0:3] = top[...].astype(f32).reshape((3, circle, channels))
    gpad[3 : own + 3] = gu[...]
    gpad[own + 3 :] = low[...].astype(f32).reshape((3, circle, channels))
    convolve(gpad, weight, out, own, True)
    gf[...] = out[...].reshape(gf.shape).astype(bf16)
    two[1]()
    for k in range(2, len(one)):
        for stream in (one, three, two):
            stream[k]()
        if k == 3:
            start_g()
    wait_sent()
    wait_r()
    wait_g()


def on_device(sizes, fields, cotangent, conv_weight, norm_gain, w_qkv, w_out):
    n_lat, n_lon, n_dp = sizes
    batch, rows, cols, channels = fields.shape
    own, circle = rows // n_lon, cols * n_lon
    att = w_out.shape[0]
    bf16, f32 = jnp.bfloat16, jnp.float32
    shape = jax.ShapeDtypeStruct
    sems = pltpu.SemaphoreType.DMA
    vmem = pltpu.VMEM
    parts = n_lat * n_lon * n_dp
    part_rows = channels // parts
    widths = (w_qkv.shape[1] // 2, w_qkv.shape[1] // 2, att + LANES)
    turns = 4 + 2 * n_lon
    blocked = (own, n_lon, cols, channels)
    flat = (own, circle, channels)
    padded = (own + 6, circle, channels)
    sums = []
    for w in widths:
        sums += [vmem((n, part_rows, w), bf16) for n in (parts, parts // 2, parts // 2, n_lon, n_lon, n_lon)]
    inside = pl.BlockSpec(memory_space=pltpu.VMEM)
    outside = pl.BlockSpec(memory_space=pl.ANY)
    result, grad_fields, one, three, two = pl.pallas_call(
        functools.partial(layer, sizes),
        out_shape=[shape((rows, cols, channels), bf16)] * 2
        + [shape((parts, part_rows, w), bf16) for w in widths],
        in_specs=[outside, outside, outside, inside, outside, outside],
        out_specs=[inside] * 5,
        scratch_shapes=[
            vmem((own + 6,) + blocked[1:], bf16), vmem(blocked, bf16), vmem(conv_weight.shape, f32),
            vmem(w_qkv.shape, bf16), vmem(w_out.shape, bf16),
            vmem(padded, f32), vmem(flat, f32), vmem(blocked, bf16), vmem(flat, f32), vmem(blocked, bf16),
            vmem(w_out.shape, f32), vmem((1, channels), f32),
            vmem((3,) + blocked[1:], bf16), vmem((3,) + blocked[1:], bf16),
            vmem(padded, f32), vmem(flat, f32), vmem(blocked, bf16), vmem(conv_weight.shape, f32),
        ] + sums + [
            sems((2, n_lon)), sems((2, n_lon)), sems((2,)), sems((2, n_lon)), sems((5,)),
            sems((2,)), sems((2,)),
            sems((n_lon,)), sems((n_lon,)), sems((n_lon,)), sems((n_lon,)),
            sems((turns,)), sems((turns,)), sems((turns,)), sems((turns,)), sems((turns,)), sems((turns,)),
        ],
        compiler_params=pltpu.CompilerParams(
            vmem_limit_bytes=67043328, collective_id=1, has_side_effects=True
        ),
    )(fields[0], cotangent[0], conv_weight, norm_gain.reshape(1, channels), w_qkv, w_out)
    outs = pl.pallas_call(
        finish,
        out_shape=[shape((rows, cols, channels), bf16)] * 2
        + [shape(w_qkv.shape, f32), shape(w_out.shape, f32), shape(conv_weight.shape, f32),
           shape((1, channels), f32)],
        in_specs=[inside] * 5,
        out_specs=[inside] * 6,
        compiler_params=pltpu.CompilerParams(vmem_limit_bytes=67043328),
    )(one, three, two, result, grad_fields)
    return outs[0][None], outs[1][None], outs[2], outs[3], outs[4], outs[5].reshape(channels)


def pick(mesh, *args):
    sizes = tuple(mesh.shape[a] for a in AXES)
    _, rows, cols, channels = args[0].shape
    att = args[5].shape[0]
    n_lat, n_lon, n_dp = sizes
    parts = n_lat * n_lon * n_dp
    fits = (
        args[0].shape[0] == 1 and n_lat == 2 and n_dp == 2 and n_lon == 4
        and rows % n_lon == 0 and rows // n_lon >= 3 and cols % 8 == 0
        and LANES % (cols * n_lon) == 0 and (rows // n_lon * cols * n_lon) % LANES == 0
        and channels == 2 * att and channels % (8 * parts) == 0 and 64 % (channels // parts) == 0
        and att % LANES == 0 and args[4].shape[1] == 3 * att and 3 * att % (2 * LANES) == 0
    )
    return on_device(sizes, *args) if fits else on_device_native(*args)


def solution(mesh):
    placed = (
        P(("member", "dp"), "lat", "lon", None),
        P(("member", "dp"), "lat", "lon", None),
        P(),
        P(),
        P(),
        P(),
    )
    return jax.shard_map(
        functools.partial(pick, mesh),
        mesh=mesh,
        in_specs=placed,
        out_specs=(
            P(("member", "dp"), "lat", "lon", None),
            P(("member", "dp"), "lat", "lon", None),
            P("member", None),
            P("member", None),
            P("member", None, None),
            P("member"),
        ),
        check_vma=False,
    )
```

profile of v0, /device:TPU:0, one launch (start us, length us, event | category | flops | bytes accessed | tf_op | source)
XLA Modules:
  0.0 65.4 jit_solution(3850749806460512398)
XLA Ops:
  0.6 61.9 %shard_map.109 = (bf16[32,8,512]{2,1,0:T(8,128)(2,1)}, bf16[32,8,512]{2,1,0:T(8,128)(2,1)}, bf16[16,32,384]{2,1,0:T(8,128)(2,1)}, bf16[16,32,384]{2,1,0:T(8,128)(2,1)}, bf16[16,32,384]{2,1,0:T(8,128)(2,1)}) custom-call(bf16[32,8,512]{2,1,0:T(8,128)(2,1)} %bitcast.6, bf16[32,8,512]{2,1,0:T(8,128)(2,1)} %bitcast.7, f32[7,7,512]{2,1,0:T(8,128)} %w_hbm.1, ...), custom_call_target="tpu_custom_call" | custom-call | tf_op jit(solution)/shard_map/pallas_call | solution.py:766
  62.5 2.9 %shard_map.110 = (bf16[32,8,512]{2,1,0:T(8,128)(2,1)}, bf16[32,8,512]{2,1,0:T(8,128)(2,1)}, f32[512,768]{1,0:T(8,128)}, f32[256,512]{1,0:T(8,128)}, f32[7,7,512]{2,1,0:T(8,128)}, /*index=5*/f32[1,512]{1,0:T(1,128)}) custom-call(bf16[16,32,384]{2,1,0:T(8,128)(2,1)} %get-tuple-element.17.one_ref, bf16[16,32,384]{2,1,0:T(8,128)(2,1)} %get-tuple-element.18.three_ref, ...), custom_call_target="tpu_custom_call" | custom-call | tf_op jit(solution)/shard_map/pallas_call | solution.py:789
where the time goes:
time: 65.6 us; the launch traced here: 65.4 us
  Pallas kernels  64.8 us (99%)
    pallas_call x1, Pallas kernels, on_device(): pl.pallas_call(functools.partial(layer, sizes), out_shape=[shape((rows, c...  61.9 us
    pallas_call x1, Pallas kernels, on_device(): pl.pallas_call(finish, out_shape=[shape((rows, cols, channels), bf16)] *...  2.92 us

commit v1 on v0

v1 whole, which is shorter than its diff:
```python
import functools
import itertools

import jax
import jax.numpy as jnp
from jax import lax
from jax.experimental import pallas as pl
from jax.experimental.pallas import tpu as pltpu
from jax.sharding import PartitionSpec as P

HEADS = 4
HEAD_DIM = 64


EPSILON = 1e-06


def with_halo(x, sides, width, wrap):
    for axis, dim in sides:
        size, length = (lax.axis_size(axis), x.shape[dim])
        up = [(i, (i + 1) % size) for i in range(size if wrap else size - 1)]
        down = [(j, i) for i, j in up]
        last = lax.slice_in_dim(x, length - width, length, axis=dim)
        first = lax.slice_in_dim(x, 0, width, axis=dim)
        before = lax.ppermute(last, axis, up)
        after = lax.ppermute(first, axis, down)
        x = jnp.concatenate([before, x, after], axis=dim)
    return x


def spread(padded, kernel, lat_rows, lon_cols):
    summed = jnp.zeros(padded.shape[:1] + (lat_rows, lon_cols, padded.shape[3]), jnp.float32)
    for row_shift in range(7):
        band = padded[:, row_shift : row_shift + lat_rows].astype(jnp.float32)
        partial_row = kernel[row_shift, 0] * band[:, :, 0:lon_cols]
        for col_shift in range(1, 7):
            partial_row = (
                partial_row
                + kernel[row_shift, col_shift] * band[:, :, col_shift : col_shift + lon_cols]
            )
        summed = summed + partial_row
    return summed


def correlate(padded, upstream, lat_rows, lon_cols):
    pieces = []
    for row_shift in range(7):
        for col_shift in range(7):
            window = padded[
                :, row_shift : row_shift + lat_rows, col_shift : col_shift + lon_cols
            ].astype(jnp.float32)
            pieces.append(jnp.sum(window * upstream, axis=(0, 1, 2)))
    return jnp.stack(pieces).reshape(7, 7, -1)


def split_heads(values):
    return values.reshape(values.shape[:-1] + (HEADS, HEAD_DIM))


def attend_forward(rowwise, att_width):
    queries = split_heads(rowwise[..., :att_width])
    keys_part = split_heads(rowwise[..., att_width : 2 * att_width])
    values_part = split_heads(rowwise[..., 2 * att_width :])
    scores = jnp.einsum(
        "brqhd,brkhd->brhqk", queries, keys_part, preferred_element_type=jnp.float32
    ) * HEAD_DIM ** (-0.5)
    row_peak = jnp.max(scores, -1, keepdims=True)
    raised = jnp.exp(scores - row_peak)
    probs = raised / jnp.sum(raised, -1, keepdims=True)
    weights = probs.astype(jnp.bfloat16)
    mixed = jnp.einsum(
        "brhqk,brkhd->brqhd", weights, values_part, preferred_element_type=jnp.float32
    )
    return (mixed.reshape(rowwise.shape[:3] + (att_width,)).astype(jnp.bfloat16), probs)


def attend_backward(rowwise, probs, grad_rowwise, att_width):
    queries = split_heads(rowwise[..., :att_width])
    keys_part = split_heads(rowwise[..., att_width : 2 * att_width])
    values_part = split_heads(rowwise[..., 2 * att_width :])
    grad_heads = split_heads(grad_rowwise)
    weights = probs.astype(jnp.bfloat16)
    grad_probs = jnp.einsum(
        "brqhd,brkhd->brhqk", grad_heads, values_part, preferred_element_type=jnp.float32
    )
    inner = jnp.sum(probs * grad_probs, -1, keepdims=True)
    grad_scores = (probs * (grad_probs - inner) * HEAD_DIM ** (-0.5)).astype(jnp.bfloat16)
    grad_query = jnp.einsum(
        "brhqk,brkhd->brqhd", grad_scores, keys_part, preferred_element_type=jnp.float32
    )
    grad_key = jnp.einsum(
        "brhqk,brqhd->brkhd", grad_scores, queries, preferred_element_type=jnp.float32
    )
    grad_value = jnp.einsum(
        "brhqk,brqhd->brkhd", weights, grad_heads, preferred_element_type=jnp.float32
    )
    shaped = rowwise.shape[:3] + (att_width,)
    return jnp.concatenate(
        [
            grad_query.reshape(shaped).astype(jnp.bfloat16),
            grad_key.reshape(shaped).astype(jnp.bfloat16),
            grad_value.reshape(shaped).astype(jnp.bfloat16),
        ],
        axis=-1,
    )


def contract_rows(left, right):
    return lax.dot_general(
        left, right, (((0,), (0,)), ((), ())), preferred_element_type=jnp.float32
    )


def contract_cols(left, right):
    return lax.dot_general(
        left, right, (((1,), (1,)), ((), ())), preferred_element_type=jnp.float32
    )


def on_device_native(fields, cotangent, conv_weight, norm_gain, w_qkv, w_out):
    batch_count, lat_rows, lon_cols, channels = fields.shape
    att_width = w_out.shape[0]
    wide = with_halo(fields, (("lon", 2),), 3, True)
    padded = with_halo(wide, (("lat", 1),), 3, False)
    update = fields.astype(jnp.float32) + spread(padded, conv_weight, lat_rows, lon_cols)
    inverse = lax.rsqrt(jnp.mean(update * update, -1, keepdims=True) + EPSILON)
    normed = (update * inverse * norm_gain).astype(jnp.bfloat16)
    normed_flat = normed.reshape(-1, channels)
    projected = jnp.dot(normed_flat, w_qkv, preferred_element_type=jnp.float32).astype(jnp.bfloat16)
    rowwise = lax.all_to_all(
        projected.reshape(batch_count, lat_rows, lon_cols, 3 * att_width),
        "lon",
        split_axis=1,
        concat_axis=2,
        tiled=True,
    )
    mixed_rows, probs = attend_forward(rowwise, att_width)
    mixed = lax.all_to_all(mixed_rows, "lon", split_axis=2, concat_axis=1, tiled=True)
    mixed_flat = mixed.reshape(-1, att_width)
    result = (
        update
        + jnp.dot(mixed_flat, w_out, preferred_element_type=jnp.float32).reshape(update.shape)
    ).astype(jnp.bfloat16)
    upstream_flat = cotangent.reshape(-1, channels)
    grad_mixed = contract_cols(upstream_flat, w_out).astype(jnp.bfloat16)
    grad_out = contract_rows(mixed_flat, upstream_flat)
    grad_rowwise = lax.all_to_all(
        grad_mixed.reshape(batch_count, lat_rows, lon_cols, att_width),
        "lon",
        split_axis=1,
        concat_axis=2,
        tiled=True,
    )
    grad_projected_rows = attend_backward(rowwise, probs, grad_rowwise, att_width)
    grad_projected = lax.all_to_all(
        grad_projected_rows, "lon", split_axis=2, concat_axis=1, tiled=True
    )
    grad_flat = grad_projected.reshape(-1, 3 * att_width)
    grad_weight = contract_rows(normed_flat, grad_flat)
    grad_normed = contract_cols(grad_flat, w_qkv).reshape(update.shape)
    grad_gain = jnp.sum(grad_normed * (update * inverse), axis=(0, 1, 2))
    gained = norm_gain * grad_normed
    grad_update = (
        cotangent.astype(jnp.float32)
        + inverse * gained
        - update * inverse**3 * jnp.mean(gained * update, -1, keepdims=True)
    )
    grad_wide = with_halo(grad_update.astype(jnp.bfloat16), (("lon", 2),), 3, True).astype(
        grad_update.dtype
    )
    grad_padded = with_halo(grad_wide.astype(jnp.bfloat16), (("lat", 1),), 3, False).astype(
        grad_wide.dtype
    )
    grad_fields = (
        grad_update + spread(grad_padded, conv_weight[::-1, ::-1], lat_rows, lon_cols)
    ).astype(jnp.bfloat16)
    grad_conv = correlate(padded, grad_update, lat_rows, lon_cols)
    totals = lax.psum((grad_weight, grad_out, grad_conv, grad_gain), ("lon", "lat", "dp"))
    return (result, grad_fields, totals[0], totals[1], totals[2], totals[3])


MESH = pl.DeviceIdType.MESH
AXES = ("lat", "lon", "dp")
LANES = 128


def place():
    return tuple(lax.axis_index(a) for a in AXES)


def greet(sizes):
    me = place()
    barrier = pltpu.get_barrier_semaphore()
    count = 0
    for offset in itertools.product(*(range(s) for s in sizes)):
        if not any(offset):
            continue
        target = {a: lax.rem(m + o, s) for a, m, o, s in zip(AXES, me, offset, sizes)}
        pl.semaphore_signal(barrier, inc=1, device_id=target, device_id_type=MESH)
        count += 1
    pl.semaphore_wait(barrier, count)


def remote(src, dst, send, recv, target):
    return pltpu.make_async_remote_copy(
        src_ref=src, dst_ref=dst, send_sem=send, recv_sem=recv, device_id=target, device_id_type=MESH
    )


def roles(own):
    lat, lon, dp = place()
    side = lon // 2
    spot = 2 * lax.rem(lon, 2) + dp

    def block(p):
        return p + lat * (3 - 2 * p)

    def owner(p):
        return {"lon": 2 * dp + p // 2, "dp": p % 2}

    def mine(p):
        return (lon == 2 * dp + p // 2) & (dp == p % 2)

    def source(i):
        return {"lon": i, "dp": side}

    def local(i):
        return (lon == i) & (dp == side)

    def rows(p):
        return pl.ds(own * block(p), own)

    return lon, spot, owner, mine, source, local, rows


def take_rows(own, src, dst, send, recv, stay):
    lon, _, owner, mine, source, local, rows = roles(own)

    def there(p):
        return remote(src.at[rows(p)], dst.at[:, lon], send.at[p], recv.at[lon], owner(p))

    def here(p, i):
        return pltpu.make_async_copy(src.at[rows(p)], dst.at[:, i], stay)

    def start():
        for p in range(4):

            @pl.when(jnp.logical_not(mine(p)))
            def _(p=p):
                there(p).start()

            @pl.when(mine(p))
            def _(p=p):
                here(p, lon).start()

    def wait():
        for i in range(4):

            @pl.when(local(i))
            def _(i=i):
                here(0, i).wait()

            @pl.when(jnp.logical_not(local(i)))
            def _(i=i):
                remote(src.at[rows(0)], dst.at[:, i], send.at[0], recv.at[i], source(i)).wait_recv()

    def wait_sent():
        for p in range(4):

            @pl.when(jnp.logical_not(mine(p)))
            def _(p=p):
                there(p).wait_send()

    return start, wait, wait_sent


def give_rows(own, src, dst, send, recv, stay):
    lon, spot, owner, mine, source, local, rows = roles(own)

    def there(i):
        return remote(src.at[:, i], dst.at[rows(spot)], send.at[i], recv.at[spot], source(i))

    def here(i):
        return pltpu.make_async_copy(src.at[:, i], dst.at[rows(spot)], stay)

    def start():
        for i in range(4):

            @pl.when(jnp.logical_not(local(i)))
            def _(i=i):
                there(i).start()

            @pl.when(local(i))
            def _(i=i):
                here(i).start()

    def wait():
        for p in range(4):

            @pl.when(jnp.logical_not(mine(p)))
            def _(p=p):
                remote(src.at[:, 0], dst.at[rows(p)], send.at[0], recv.at[p], owner(p)).wait_recv()

        for i in range(4):

            @pl.when(jnp.logical_not(local(i)))
            def _(i=i):
                there(i).wait_send()

            @pl.when(local(i))
            def _(i=i):
                here(i).wait()

    return start, wait


def halo_rows(first, last, top, low, send, recv):
    lat, lon, dp = place()
    side = lon // 2
    spot = 2 * lax.rem(lon, 2) + dp
    index, end = 4 * lat + spot + lat * (3 - 2 * spot), 7

    def at(k):
        k = lax.rem(k + 8, 8)
        band = k // 4
        b = lax.rem(k, 4)
        p = b + band * (3 - 2 * b)
        return {"lat": band, "lon": 2 * side + p // 2, "dp": lax.rem(p, 2)}

    down = remote(last, top, send.at[0], recv.at[0], at(index + 1))
    up = remote(first, low, send.at[1], recv.at[1], at(index + 7))

    def start():
        @pl.when(index < end)
        def _():
            down.start()

        @pl.when(index > 0)
        def _():
            up.start()

        @pl.when(index == 0)
        def _():
            top[...] = jnp.zeros(top.shape, top.dtype)

        @pl.when(index == end)
        def _():
            low[...] = jnp.zeros(low.shape, low.dtype)

    def wait():
        @pl.when(index > 0)
        def _():
            down.wait_recv()
            up.wait_send()

        @pl.when(index < end)
        def _():
            up.wait_recv()
            down.wait_send()

    return start, wait


def convolve(pad, weight, out, own, flip, halo):
    circle, channels = pad.shape[1], pad.shape[2]
    taken = {}
    for r in range(own):
        taps = [a for a in range(7) if (3 <= r + a < own + 3) != halo]
        if taps:
            taken[r] = taps

    def chunk(c, carry):
        lanes = pl.ds(pl.multiple_of(c * LANES, LANES), LANES)
        totals = {r: out[r, :, lanes] if halo else pad[r + 3, :, lanes] for r in taken}
        for e in range(7):
            turn = (3 - e) % circle
            column = 6 - e if flip else e
            taps = [weight[6 - a if flip else a, column : column + 1, lanes] for a in range(7)]
            for r in taken:
                part = None
                for a in taken[r]:
                    term = pad[r + a, :, lanes] * taps[a]
                    part = term if part is None else part + term
                if turn:
                    part = pltpu.roll(part, turn, 0)
                totals[r] = totals[r] + part
        for r in taken:
            out[r, :, lanes] = totals[r]
        return carry

    lax.fori_loop(0, channels // LANES, chunk, 0)


def correlate_rows(pad, upstream, out, own, low, high):
    circle = pad.shape[1]

    def chunk(c, carry):
        lanes = pl.ds(pl.multiple_of(c * LANES, LANES), LANES)
        for e in range(7):
            turn = (e - 3) % circle
            turned = [upstream[r, :, lanes] for r in range(own)]
            if turn:
                turned = [pltpu.roll(t, turn, 0) for t in turned]
            for a in range(7):
                total = None
                for r in range(own):
                    term = pad[r + a, :, lanes] * turned[r]
                    total = term if total is None else total + term
                out[a, e : e + 1, lanes] = jnp.sum(total, axis=0, keepdims=True)
        return carry

    lax.fori_loop(low, high, chunk, 0)


def dot(left, right, dims):
    return lax.dot_general(left, right, (dims, ((), ())), preferred_element_type=jnp.float32)


PLAIN, COLS, ROWS = ((1,), (0,)), ((1,), (1,)), ((0,), (0,))


def attend_rows(projected, circle, att_width):
    cells = projected.shape[0]
    group = max(circle, LANES)
    row_of = lax.broadcasted_iota(jnp.int32, (group, group), 0) // circle
    col_of = lax.broadcasted_iota(jnp.int32, (group, group), 1) // circle
    same = row_of == col_of
    lane_head = lax.broadcasted_iota(jnp.int32, (group, LANES), 1) // HEAD_DIM
    bf16 = jnp.bfloat16
    zero = jnp.zeros((), bf16)
    heads = range(LANES // HEAD_DIM)
    groups = [slice(g * group, (g + 1) * group) for g in range(cells // group)]
    pairs = [slice(p * LANES, (p + 1) * LANES) for p in range(att_width // LANES)]

    def third(k, cut, at):
        return projected[cut, k * att_width : (k + 1) * att_width][:, at]

    def join(parts):
        whole = parts[0]
        for h in heads[1:]:
            whole = jnp.where(lane_head == h, parts[h], whole)
        return whole.astype(bf16)

    kept, mixed = {}, []
    for g, cut in enumerate(groups):
        found = []
        for p, at in enumerate(pairs):
            q, k, v = (third(n, cut, at) for n in range(3))
            parts = []
            for h in heads:
                scores = dot(jnp.where(lane_head == h, q, zero), k, COLS) * HEAD_DIM ** (-0.5)
                scores = jnp.where(same, scores, -jnp.inf)
                raised = jnp.exp(scores - jnp.max(scores, -1, keepdims=True))
                probs = raised / jnp.sum(raised, -1, keepdims=True)
                kept[g, p, h] = probs
                parts.append(dot(probs.astype(bf16), v, PLAIN))
            found.append(join(parts))
        mixed.append(jnp.concatenate(found, axis=1))

    def backward(grad_mixed):
        grads = []
        for g, cut in enumerate(groups):
            found = [[], [], []]
            for p, at in enumerate(pairs):
                q, k, v = (third(n, cut, at) for n in range(3))
                up = grad_mixed[cut, at]
                parts = [[], [], []]
                for h in heads:
                    probs = kept[g, p, h]
                    grad_probs = dot(jnp.where(lane_head == h, up, zero), v, COLS)
                    inner = jnp.sum(probs * grad_probs, -1, keepdims=True)
                    grad_scores = (probs * (grad_probs - inner) * HEAD_DIM ** (-0.5)).astype(bf16)
                    parts[0].append(dot(grad_scores, k, PLAIN))
                    parts[1].append(dot(grad_scores, q, ROWS))
                    parts[2].append(dot(probs.astype(bf16), up, ROWS))
                for part, into in zip(parts, found):
                    into.append(join(part))
            grads.append(jnp.concatenate(found[0] + found[1] + found[2], axis=1))
        return jnp.concatenate(grads, axis=0)

    return jnp.concatenate(mixed, axis=0), backward


def core_step(cr_ref, update_ref, gain, wq_ref, wo_ref, result_ref, gu_ref, gub_ref, bq_refs, bo_ref, gg_ref):
    own, blocks, width, channels = cr_ref.shape
    circle, cells = blocks * width, own * blocks * width
    att_width = wo_ref.shape[0]
    bf16 = jnp.bfloat16
    update = update_ref[...].reshape(cells, channels)
    inverse = lax.rsqrt(jnp.mean(update * update, -1, keepdims=True) + EPSILON)
    normed = (update * inverse * gain).astype(bf16)
    projected = dot(normed, wq_ref[...], PLAIN).astype(bf16)
    mixed, backward = attend_rows(projected, circle, att_width)
    result = update + dot(mixed, wo_ref[...], PLAIN)
    result_ref[...] = result.reshape(result_ref.shape).astype(bf16)
    yield
    cot32 = cr_ref[...].astype(jnp.float32).reshape(cells, channels)
    cot = cot32.astype(bf16)
    bo_ref[...] = dot(mixed, cot, ROWS).astype(bf16).reshape(bo_ref.shape)
    yield
    grad_mixed = dot(cot, wo_ref[...], COLS).astype(bf16)
    grad_projected = backward(grad_mixed)
    grad_normed = dot(grad_projected, wq_ref[...], COLS)
    gained = gain * grad_normed
    grad_update = (
        cot32
        + inverse * gained
        - update * (inverse * inverse * inverse) * jnp.mean(gained * update, -1, keepdims=True)
    )
    gu_ref[...] = grad_update.reshape(gu_ref.shape)
    gub_ref[...] = grad_update.reshape(gub_ref.shape).astype(bf16)
    yield
    for k, ref in enumerate(bq_refs):
        part = ref.shape[2]
        piece = dot(normed, grad_projected[:, k * part : (k + 1) * part], ROWS)
        ref[...] = piece.astype(bf16).reshape(ref.shape)
    yield
    gg_ref[...] = jnp.sum(grad_normed * (update * inverse), axis=0, keepdims=True)
    yield


def pack_small(big, conv, gg_ref):
    channels = gg_ref.shape[1]
    fill = big.shape[0] * big.shape[1] - 50
    small = jnp.concatenate(
        [conv[a] for a in range(7)] + [gg_ref[...], jnp.zeros((fill, channels), jnp.float32)], axis=0
    )
    big[...] = small.astype(jnp.bfloat16).reshape(big.shape)


def finish(*refs):
    every, outs = refs[: len(refs) - 6], refs[len(refs) - 6 :]
    result_ref, gf_ref, out_ref, small_ref = every[:4]
    result_out, gf_out, gq_out, go_out, gc_out, gg_out = outs
    f32 = jnp.float32
    result_out[...] = result_ref[...]
    gf_out[...] = gf_ref[...]
    for k, ref in enumerate(every[4:]):
        part = ref.shape[2]
        gq_out[:, k * part : (k + 1) * part] = ref[...].astype(f32).reshape(gq_out.shape[0], part)
    go_out[...] = out_ref[...].astype(f32).reshape(go_out.shape)
    small = small_ref[...].astype(f32).reshape(-1, go_out.shape[1])
    for a in range(7):
        gc_out[a] = small[a * 7 : (a + 1) * 7]
    gg_out[...] = small[49:50]


def sum_stages(big, every, got1, sum1, got2, sum2, got3, sum3, got4, send, recv):
    lat, lon, dp = place()
    f32 = jnp.float32
    other_dp, other_lat = 1 - dp, 1 - lat
    half = lon // 2
    inner = (lon == 1) | (lon == 2)
    outer = jnp.logical_not(inner)
    mine, across = every.at[2 * dp + lat], every.at[2 * dp + other_lat]
    core = remote(big.at[pl.ds(2 * other_dp, 2)], got1, send.at[0], recv.at[0], {"dp": other_dp})
    band = remote(sum1.at[other_lat], got2, send.at[1], recv.at[1], {"lat": other_lat})
    inward = remote(sum2, got3, send.at[2], recv.at[2], {"lon": 1 + half})
    middle = remote(sum3, got4, send.at[3], recv.at[3], {"lon": 3 - lon})
    out_band = remote(mine, mine, send.at[4], recv.at[4], {"lat": other_lat})
    out_lon = remote(mine, mine, send.at[5], recv.at[5], {"lon": 3 * half})
    out_both = remote(mine, mine, send.at[6], recv.at[6], {"lat": other_lat, "lon": 3 * half})
    in_band = remote(across, across, send.at[4], recv.at[4], {"lat": other_lat})
    in_both = remote(across, across, send.at[6], recv.at[6], {"lat": other_lat, "lon": 1 + half})
    ours, theirs = every.at[pl.ds(2 * dp, 2)], every.at[pl.ds(2 * other_dp, 2)]
    out_core = remote(ours, ours, send.at[7], recv.at[7], {"dp": other_dp})
    in_core = remote(theirs, theirs, send.at[7], recv.at[7], {"dp": other_dp})

    def add(a, b, to):
        to[...] = (a[...].astype(f32) + b[...].astype(f32)).astype(to.dtype)

    def s0():
        core.start()

    def s1():
        core.wait()
        add(big.at[pl.ds(2 * dp, 2)], got1, sum1)
        band.start()

    def s2():
        band.wait()
        add(sum1.at[lat], got2, sum2)

        @pl.when(outer)
        def _():
            inward.start()

    def s3():
        @pl.when(inner)
        def _():
            inward.wait_recv()
            add(sum2, got3, sum3)
            middle.start()

    def s4():
        @pl.when(inner)
        def _():
            middle.wait()
            add(sum3, got4, mine)
            out_lon.start()
            out_both.start()
            out_band.start()

    def s5():
        @pl.when(inner)
        def _():
            in_band.wait_recv()
            out_core.start()

        @pl.when(outer)
        def _():
            out_lon.wait_recv()
            in_both.wait_recv()
            out_core.start()

    def s6():
        out_core.wait_send()
        in_core.wait_recv()

        @pl.when(inner)
        def _():
            out_lon.wait_send()
            out_both.wait_send()
            out_band.wait_send()

        @pl.when(outer)
        def _():
            inward.wait_send()

    return s0, s1, s2, s3, s4, s5, s6


def layer(sizes, f_ref, c_ref, w_hbm, gain_ref, wq_hbm, wo_hbm, result_out, gf_out, *rest):
    every, rest = rest[:STREAMS], rest[STREAMS:]
    (fp, cr, weight, wq, wo, pad, update, result, gpad, gub, gg, low, out, gf, conv,
     f_send, f_recv, c_send, c_recv, stay, fh_send, fh_recv, gh_send, gh_recv,
     r_send, r_recv, g_send, g_recv), rest = rest[:28], rest[28:]
    own, circle, channels = update.shape
    f32, bf16 = jnp.float32, jnp.bfloat16
    loads = [
        pltpu.make_async_copy(src, dst, stay.at[k])
        for k, (src, dst) in enumerate(((w_hbm, weight), (wq_hbm, wq), (wo_hbm, wo)))
    ]
    for load in loads:
        load.start()
    per = len(rest) // STREAMS
    bigs = [rest[k * per] for k in range(STREAMS)]
    streams = [sum_stages(bigs[k], every[k], *rest[k * per + 1 : (k + 1) * per - 2], *rest[(k + 1) * per - 2 : (k + 1) * per])
               for k in range(STREAMS)]
    head, small, body = streams[0], streams[1], streams[2:]
    start_f, wait_f, sent_f = take_rows(own, f_ref, fp.at[pl.ds(3, own)], f_send, f_recv, stay.at[3])
    start_c, wait_c, sent_c = take_rows(own, c_ref, cr, c_send, c_recv, stay.at[4])
    start_fh, wait_fh = halo_rows(
        fp.at[pl.ds(3, 3)], fp.at[pl.ds(own, 3)], fp.at[pl.ds(0, 3)], fp.at[pl.ds(own + 3, 3)], fh_send, fh_recv
    )
    start_gh, wait_gh = halo_rows(
        gub.at[pl.ds(0, 3)], gub.at[pl.ds(own - 3, 3)], low.at[pl.ds(0, 3)], low.at[pl.ds(3, 3)], gh_send, gh_recv
    )
    start_r, wait_r = give_rows(own, result, result_out, r_send, r_recv, stay.at[5])
    start_g, wait_g = give_rows(own, gf, gf_out, g_send, g_recv, stay.at[6])

    def widen(src, at, rows, dst, to):
        dst[to : to + rows] = src[at : at + rows].astype(f32).reshape((rows, circle, channels))

    greet(sizes)
    start_f()
    for load in loads:
        load.wait()
    wait_f()
    start_fh()
    start_c()
    widen(fp, 3, own, pad, 3)
    convolve(pad, weight, update, own, False, False)
    wait_fh()
    widen(fp, 0, 3, pad, 0)
    widen(fp, own + 3, 3, pad, own + 3)
    convolve(pad, weight, update, own, False, True)
    steps = core_step(
        cr, update, gain_ref[...], wq, wo, result, gpad.at[pl.ds(3, own)], gub, bigs[2:], bigs[0], gg
    )
    next(steps)
    start_r()
    wait_c()
    next(steps)
    head[0]()
    next(steps)
    start_gh()
    next(steps)
    for stream in body:
        stream[0]()
    head[1]()
    next(steps)
    correlate_rows(pad, gpad.at[pl.ds(3, own)], conv, own, 0, 2)
    for stream in body:
        stream[1]()
    correlate_rows(pad, gpad.at[pl.ds(3, own)], conv, own, 2, channels // LANES)
    pack_small(bigs[1], conv, gg)
    small[0]()
    head[2]()
    convolve(gpad, weight, out, own, True, False)
    small[1]()
    for stream in body:
        stream[2]()
    head[3]()
    wait_gh()
    widen(low, 0, 3, gpad, 0)
    widen(low, 3, 3, gpad, own + 3)
    convolve(gpad, weight, out, own, True, True)
    gf[...] = out[...].reshape(gf.shape).astype(bf16)
    start_g()
    for k in range(2, len(small)):
        small[k]()
        if k + 1 < len(small):
            for stream in body:
                stream[k + 1]()
        if k + 2 < len(small):
            head[k + 2]()
    sent_f()
    sent_c()
    wait_r()
    wait_g()


STREAMS = 5


def on_device(sizes, fields, cotangent, conv_weight, norm_gain, w_qkv, w_out):
    n_lat, n_lon, n_dp = sizes
    batch, rows, cols, channels = fields.shape
    own, circle = rows // n_lon, cols * n_lon
    att = w_out.shape[0]
    bf16, f32 = jnp.bfloat16, jnp.float32
    shape = jax.ShapeDtypeStruct
    sems = pltpu.SemaphoreType.DMA
    vmem = pltpu.VMEM
    third = w_qkv.shape[1] // 3
    pieces = [(att // 4, channels), (16, channels)] + [(channels // 4, third)] * 3
    blocked = (own, n_lon, cols, channels)
    flat = (own, circle, channels)
    padded = (own + 6, circle, channels)
    sums = []
    for r, w in pieces:
        sums += [vmem((n, r, w), bf16) for n in (4, 2, 2)] + [vmem((r, w), bf16)] * 5
        sums += [sems((8,)), sems((8,))]
    inside = pl.BlockSpec(memory_space=pltpu.VMEM)
    outside = pl.BlockSpec(memory_space=pl.ANY)
    outs = pl.pallas_call(
        functools.partial(layer, sizes),
        out_shape=[shape((rows, cols, channels), bf16)] * 2 + [shape((4, r, w), bf16) for r, w in pieces],
        in_specs=[outside, outside, outside, inside, outside, outside],
        out_specs=[outside] * 2 + [inside] * STREAMS,
        scratch_shapes=[
            vmem((own + 6,) + blocked[1:], bf16), vmem(blocked, bf16), vmem(conv_weight.shape, f32),
            vmem(w_qkv.shape, bf16), vmem(w_out.shape, bf16),
            vmem(padded, f32), vmem(flat, f32), vmem(blocked, bf16), vmem(padded, f32), vmem(blocked, bf16),
            vmem((1, channels), f32), vmem((6,) + blocked[1:], bf16), vmem(flat, f32), vmem(blocked, bf16),
            vmem(conv_weight.shape, f32),
            sems((4,)), sems((4,)), sems((4,)), sems((4,)), sems((7,)), sems((2,)), sems((2,)), sems((2,)), sems((2,)),
            sems((4,)), sems((4,)), sems((4,)), sems((4,)),
        ] + sums,
        compiler_params=pltpu.CompilerParams(
            vmem_limit_bytes=67043328, collective_id=1, has_side_effects=True
        ),
    )(fields[0], cotangent[0], conv_weight, norm_gain.reshape(1, channels), w_qkv, w_out)
    outs = pl.pallas_call(
        finish,
        out_shape=[shape((rows, cols, channels), bf16)] * 2
        + [shape(w_qkv.shape, f32), shape(w_out.shape, f32), shape(conv_weight.shape, f32),
           shape((1, channels), f32)],
        in_specs=[inside] * len(outs),
        out_specs=[inside] * 6,
        compiler_params=pltpu.CompilerParams(vmem_limit_bytes=67043328),
    )(*outs)
    return outs[0][None], outs[1][None], outs[2], outs[3], outs[4], outs[5].reshape(channels)


def pick(mesh, *args):
    sizes = tuple(mesh.shape[a] for a in AXES)
    _, rows, cols, channels = args[0].shape
    att = args[5].shape[0]
    n_lat, n_lon, n_dp = sizes
    fits = (
        args[0].shape[0] == 1 and n_lat == 2 and n_dp == 2 and n_lon == 4
        and rows % n_lon == 0 and rows // n_lon >= 3 and cols % 8 == 0
        and LANES % (cols * n_lon) == 0 and (rows // n_lon * cols * n_lon) % LANES == 0
        and args[2].shape[:2] == (7, 7) and channels % LANES == 0 and att % LANES == 0
        and args[4].shape[1] == 3 * att
    )
    return on_device(sizes, *args) if fits else on_device_native(*args)


def solution(mesh):
    placed = (
        P(("member", "dp"), "lat", "lon", None),
        P(("member", "dp"), "lat", "lon", None),
        P(),
        P(),
        P(),
        P(),
    )
    return jax.shard_map(
        functools.partial(pick, mesh),
        mesh=mesh,
        in_specs=placed,
        out_specs=(
            P(("member", "dp"), "lat", "lon", None),
            P(("member", "dp"), "lat", "lon", None),
            P("member", None),
            P("member", None),
            P("member", None, None),
            P("member"),
        ),
        check_vma=False,
    )
```

time: 65.6 us -> 61.5 us (0.938)
  Pallas kernels: 64.8 us -> 60.6 us
    pallas_call x1, Pallas kernels: 61.9 us -> 57.7 us  [on_device(): pl.pallas_call(functools.partial(layer, sizes), out_shape=[shape((rows, c...]
where the time goes in v1:
time: 61.5 us; the launch traced here: 61.3 us
  Pallas kernels  60.6 us (99%)
  between operations  0.64 us (1%)
    pallas_call x1, Pallas kernels, on_device(): pl.pallas_call(functools.partial(layer, sizes), out_shape=[shape((rows, c...  57.7 us
    pallas_call x1, Pallas kernels, on_device(): pl.pallas_call(finish, out_shape=[shape((rows, cols, channels), bf16)] *...  2.91 us

profile of v1, /device:TPU:0, one launch (start us, length us, event | category | flops | bytes accessed | tf_op | source)
XLA Modules:
  0.0 61.3 jit_solution(17907124729707746595)
XLA Ops:
  0.6 57.7 %shard_map.109 = (bf16[32,8,512]{2,1,0:T(8,128)(2,1)}, bf16[32,8,512]{2,1,0:T(8,128)(2,1)}, bf16[4,64,512]{2,1,0:T(8,128)(2,1)}, bf16[4,16,512]{2,1,0:T(8,128)(2...) custom-call(bf16[32,8,512]{2,1,0:T(8,128)(2,1)} %bitcast.6, ...), custom_call_target="tpu_custom_call" | custom-call | tf_op jit(solution)/shard_map/pallas_call | solution.py:747
  58.4 2.9 %shard_map.110 = (bf16[32,8,512]{2,1,0:T(8,128)(2,1)}, bf16[32,8,512]{2,1,0:T(8,128)(2,1)}, f32[512,768]{1,0:T(8,128)}, f32[256,512]{1,0:T(8,128)}, f32[7,7,512]{2,1,0:T(8,128)}, /*index=5*/f32[1,512]{1,0:T(1,128)}) custom-call(bf16[32,8,512]{2,1,0:T(8,128)(2,1)} %get-tuple-element.19.refs_0_, bf16[32,8,512]{2,1,0:T(8,128)(2,1)} %get-tuple-element.20.refs_1_, ...), custom_call_target="tpu_custom_call" | custom-call | tf_op jit(solution)/shard_map/pallas_call | solution.py:765

commit v2 on v1

--- a/solution.py
+++ b/solution.py
@@ -193,7 +193,7 @@
     barrier = pltpu.get_barrier_semaphore()
     count = 0
     for offset in itertools.product(*(range(s) for s in sizes)):
-        if not any(offset):
+        if not any(offset) or (offset[0] and any(offset[1:])):
             continue
         target = {a: lax.rem(m + o, s) for a, m, o, s in zip(AXES, me, offset, sizes)}
         pl.semaphore_signal(barrier, inc=1, device_id=target, device_id_type=MESH)
@@ -207,7 +207,7 @@
     )
 
 
-def roles(own):
+def roles(own, low, count):
     lat, lon, dp = place()
     side = lon // 2
     spot = 2 * lax.rem(lon, 2) + dp
@@ -228,13 +228,13 @@
         return (lon == i) & (dp == side)
 
     def rows(p):
-        return pl.ds(own * block(p), own)
+        return pl.ds(own * block(p) + low, count)
 
     return lon, spot, owner, mine, source, local, rows
 
 
 def take_rows(own, src, dst, send, recv, stay):
-    lon, _, owner, mine, source, local, rows = roles(own)
+    lon, _, owner, mine, source, local, rows = roles(own, 0, own)
 
     def there(p):
         return remote(src.at[rows(p)], dst.at[:, lon], send.at[p], recv.at[lon], owner(p))
@@ -274,14 +274,15 @@
     return start, wait, wait_sent
 
 
-def give_rows(own, src, dst, send, recv, stay):
-    lon, spot, owner, mine, source, local, rows = roles(own)
+def give_rows(own, low, count, src, dst, send, recv, stay):
+    lon, spot, owner, mine, source, local, rows = roles(own, low, count)
+    part = src.at[pl.ds(low, count)]
 
     def there(i):
-        return remote(src.at[:, i], dst.at[rows(spot)], send.at[i], recv.at[spot], source(i))
+        return remote(part.at[:, i], dst.at[rows(spot)], send.at[i], recv.at[spot], source(i))
 
     def here(i):
-        return pltpu.make_async_copy(src.at[:, i], dst.at[rows(spot)], stay)
+        return pltpu.make_async_copy(part.at[:, i], dst.at[rows(spot)], stay)
 
     def start():
         for i in range(4):
@@ -299,7 +300,7 @@
 
             @pl.when(jnp.logical_not(mine(p)))
             def _(p=p):
-                remote(src.at[:, 0], dst.at[rows(p)], send.at[0], recv.at[p], owner(p)).wait_recv()
+                remote(part.at[:, 0], dst.at[rows(p)], send.at[0], recv.at[p], owner(p)).wait_recv()
 
         for i in range(4):
 
@@ -500,6 +501,11 @@
     yield
     grad_mixed = dot(cot, wo_ref[...], COLS).astype(bf16)
     grad_projected = backward(grad_mixed)
+    for k, ref in enumerate(bq_refs):
+        part = ref.shape[2]
+        piece = dot(normed, grad_projected[:, k * part : (k + 1) * part], ROWS)
+        ref[...] = piece.astype(bf16).reshape(ref.shape)
+    yield
     grad_normed = dot(grad_projected, wq_ref[...], COLS)
     gained = gain * grad_normed
     grad_update = (
@@ -509,11 +515,6 @@
     )
     gu_ref[...] = grad_update.reshape(gu_ref.shape)
     gub_ref[...] = grad_update.reshape(gub_ref.shape).astype(bf16)
-    yield
-    for k, ref in enumerate(bq_refs):
-        part = ref.shape[2]
-        piece = dot(normed, grad_projected[:, k * part : (k + 1) * part], ROWS)
-        ref[...] = piece.astype(bf16).reshape(ref.shape)
     yield
     gg_ref[...] = jnp.sum(grad_normed * (update * inverse), axis=0, keepdims=True)
     yield
@@ -557,14 +558,12 @@
     band = remote(sum1.at[other_lat], got2, send.at[1], recv.at[1], {"lat": other_lat})
     inward = remote(sum2, got3, send.at[2], recv.at[2], {"lon": 1 + half})
     middle = remote(sum3, got4, send.at[3], recv.at[3], {"lon": 3 - lon})
-    out_band = remote(mine, mine, send.at[4], recv.at[4], {"lat": other_lat})
-    out_lon = remote(mine, mine, send.at[5], recv.at[5], {"lon": 3 * half})
-    out_both = remote(mine, mine, send.at[6], recv.at[6], {"lat": other_lat, "lon": 3 * half})
-    in_band = remote(across, across, send.at[4], recv.at[4], {"lat": other_lat})
-    in_both = remote(across, across, send.at[6], recv.at[6], {"lat": other_lat, "lon": 1 + half})
+    outward = remote(mine, mine, send.at[4], recv.at[4], {"lon": 3 * half})
+    out_band = remote(mine, mine, send.at[5], recv.at[5], {"lat": other_lat})
+    in_band = remote(across, across, send.at[5], recv.at[5], {"lat": other_lat})
     ours, theirs = every.at[pl.ds(2 * dp, 2)], every.at[pl.ds(2 * other_dp, 2)]
-    out_core = remote(ours, ours, send.at[7], recv.at[7], {"dp": other_dp})
-    in_core = remote(theirs, theirs, send.at[7], recv.at[7], {"dp": other_dp})
+    out_core = remote(ours, ours, send.at[6], recv.at[6], {"dp": other_dp})
+    in_core = remote(theirs, theirs, send.at[6], recv.at[6], {"dp": other_dp})
 
     def add(a, b, to):
         to[...] = (a[...].astype(f32) + b[...].astype(f32)).astype(to.dtype)
@@ -597,35 +596,85 @@
         def _():
             middle.wait()
             add(sum3, got4, mine)
-            out_lon.start()
-            out_both.start()
+            outward.start()
             out_band.start()
 
     def s5():
-        @pl.when(inner)
-        def _():
-            in_band.wait_recv()
-            out_core.start()
-
         @pl.when(outer)
         def _():
-            out_lon.wait_recv()
-            in_both.wait_recv()
-            out_core.start()
+            outward.wait_recv()
+            out_band.start()
 
     def s6():
+        in_band.wait_recv()
+        out_core.start()
+
+    def s7():
         out_core.wait_send()
         in_core.wait_recv()
+        out_band.wait_send()
 
         @pl.when(inner)
         def _():
-            out_lon.wait_send()
-            out_both.wait_send()
-            out_band.wait_send()
+            outward.wait_send()
 
         @pl.when(outer)
         def _():
             inward.wait_send()
+
+    return s0, s1, s2, s3, s4, s5, s6, s7
+
+
+def sum_stages_near(big, every, got1, sum1, got2, sum2, got3, sum3, got4, send, recv):
+    lat, lon, dp = place()
+    f32 = jnp.float32
+    other_dp, other_lat = 1 - dp, 1 - lat
+    near, far = lon + 1 - 2 * lax.rem(lon, 2), lax.rem(lon + 2, 4)
+    mine, across = every.at[2 * dp + lat], every.at[2 * dp + other_lat]
+    core = remote(big.at[pl.ds(2 * other_dp, 2)], got1, send.at[0], recv.at[0], {"dp": other_dp})
+    band = remote(sum1.at[other_lat], got2, send.at[1], recv.at[1], {"lat": other_lat})
+    one = remote(sum2, got3, send.at[2], recv.at[2], {"lon": near})
+    two = remote(sum3, got4, send.at[3], recv.at[3], {"lon": far})
+    out_band = remote(mine, mine, send.at[4], recv.at[4], {"lat": other_lat})
+    in_band = remote(across, across, send.at[4], recv.at[4], {"lat": other_lat})
+    ours, theirs = every.at[pl.ds(2 * dp, 2)], every.at[pl.ds(2 * other_dp, 2)]
+    out_core = remote(ours, ours, send.at[5], recv.at[5], {"dp": other_dp})
+    in_core = remote(theirs, theirs, send.at[5], recv.at[5], {"dp": other_dp})
+
+    def add(a, b, to):
+        to[...] = (a[...].astype(f32) + b[...].astype(f32)).astype(to.dtype)
+
+    def s0():
+        core.start()
+
+    def s1():
+        core.wait_recv()
+        add(big.at[pl.ds(2 * dp, 2)], got1, sum1)
+        band.start()
+
+    def s2():
+        band.wait_recv()
+        add(sum1.at[lat], got2, sum2)
+        one.start()
+
+    def s3():
+        one.wait_recv()
+        add(sum2, got3, sum3)
+        two.start()
+
+    def s4():
+        two.wait_recv()
+        add(sum3, got4, mine)
+        out_band.start()
+
+    def s5():
+        in_band.wait_recv()
+        out_core.start()
+
+    def s6():
+        in_core.wait_recv()
+        for copy in (core, band, one, two, out_band, out_core):
+            copy.wait_send()
 
     return s0, s1, s2, s3, s4, s5, s6
 
@@ -645,8 +694,10 @@
         load.start()
     per = len(rest) // STREAMS
     bigs = [rest[k * per] for k in range(STREAMS)]
-    streams = [sum_stages(bigs[k], every[k], *rest[k * per + 1 : (k + 1) * per - 2], *rest[(k + 1) * per - 2 : (k + 1) * per])
-               for k in range(STREAMS)]
+    streams = []
+    for k in range(STREAMS):
+        refs = rest[k * per : (k + 1) * per]
+        streams.append((sum_stages_near if k == 1 else sum_stages)(refs[0], every[k], *refs[1:]))
     head, small, body = streams[0], streams[1], streams[2:]
     start_f, wait_f, sent_f = take_rows(own, f_ref, fp.at[pl.ds(3, own)], f_send, f_recv, stay.at[3])
     start_c, wait_c, sent_c = take_rows(own, c_ref, cr, c_send, c_recv, stay.at[4])
@@ -656,9 +707,11 @@
     start_gh, wait_gh = halo_rows(
         gub.at[pl.ds(0, 3)], gub.at[pl.ds(own - 3, 3)], low.at[pl.ds(0, 3)], low.at[pl.ds(3, 3)], gh_send, gh_recv
     )
-    start_r, wait_r = give_rows(own, result, result_out, r_send, r_recv, stay.at[5])
-    start_g, wait_g = give_rows(own, gf, gf_out, g_send, g_recv, stay.at[6])
-
+    cut = own // 2
+    returns = []
+    for src, dst, send, recv, at in ((result, result_out, r_send, r_recv, 5), (gf, gf_out, g_send, g_recv, 7)):
+        for k, (low_row, count) in enumerate(((0, cut), (cut, own - cut))):
+            returns.append(give_rows(own, low_row, count, src, dst, send.at[k], recv.at[k], stay.at[at + k]))
     def widen(src, at, rows, dst, to):
         dst[to : to + rows] = src[at : at + rows].astype(f32).reshape((rows, circle, channels))
 
@@ -679,21 +732,21 @@
         cr, update, gain_ref[...], wq, wo, result, gpad.at[pl.ds(3, own)], gub, bigs[2:], bigs[0], gg
     )
     next(steps)
-    start_r()
+    returns[0][0]()
     wait_c()
     next(steps)
     head[0]()
-    next(steps)
-    start_gh()
     next(steps)
     for stream in body:
         stream[0]()
     head[1]()
     next(steps)
-    correlate_rows(pad, gpad.at[pl.ds(3, own)], conv, own, 0, 2)
+    start_gh()
+    returns[1][0]()
     for stream in body:
         stream[1]()
-    correlate_rows(pad, gpad.at[pl.ds(3, own)], conv, own, 2, channels // LANES)
+    next(steps)
+    correlate_rows(pad, gpad.at[pl.ds(3, own)], conv, own, 0, channels // LANES)
     pack_small(bigs[1], conv, gg)
     small[0]()
     head[2]()
@@ -707,21 +760,23 @@
     widen(low, 3, 3, gpad, own + 3)
     convolve(gpad, weight, out, own, True, True)
     gf[...] = out[...].reshape(gf.shape).astype(bf16)
-    start_g()
-    for k in range(2, len(small)):
-        small[k]()
-        if k + 1 < len(small):
-            for stream in body:
-                stream[k + 1]()
-        if k + 2 < len(small):
-            head[k + 2]()
+    for k in range(3, 8):
+        small[k - 1]()
+        for stream in body:
+            stream[k]()
+        if k + 1 < 8:
+            head[k + 1]()
+        if k == 4:
+            returns[2][0]()
+        if k == 4:
+            returns[3][0]()
     sent_f()
     sent_c()
-    wait_r()
-    wait_g()
-
-
-STREAMS = 5
+    for _, wait in returns:
+        wait()
+
+
+STREAMS = 8
 
 
 def on_device(sizes, fields, cotangent, conv_weight, norm_gain, w_qkv, w_out):
@@ -733,8 +788,8 @@
     shape = jax.ShapeDtypeStruct
     sems = pltpu.SemaphoreType.DMA
     vmem = pltpu.VMEM
-    third = w_qkv.shape[1] // 3
-    pieces = [(att // 4, channels), (16, channels)] + [(channels // 4, third)] * 3
+    width = w_qkv.shape[1] // (STREAMS - 2)
+    pieces = [(att // 4, channels), (16, channels)] + [(channels // 4, width)] * (STREAMS - 2)
     blocked = (own, n_lon, cols, channels)
     flat = (own, circle, channels)
     padded = (own + 6, circle, channels)
@@ -755,8 +810,8 @@
             vmem(padded, f32), vmem(flat, f32), vmem(blocked, bf16), vmem(padded, f32), vmem(blocked, bf16),
             vmem((1, channels), f32), vmem((6,) + blocked[1:], bf16), vmem(flat, f32), vmem(blocked, bf16),
             vmem(conv_weight.shape, f32),
-            sems((4,)), sems((4,)), sems((4,)), sems((4,)), sems((7,)), sems((2,)), sems((2,)), sems((2,)), sems((2,)),
-            sems((4,)), sems((4,)), sems((4,)), sems((4,)),
+            sems((4,)), sems((4,)), sems((4,)), sems((4,)), sems((9,)), sems((2,)), sems((2,)), sems((2,)), sems((2,)),
+            sems((2, 4)), sems((2, 4)), sems((2, 4)), sems((2, 4)),
         ] + sums,
         compiler_params=pltpu.CompilerParams(
             vmem_limit_bytes=67043328, collective_id=1, has_side_effects=True
@@ -784,7 +839,7 @@
         and rows % n_lon == 0 and rows // n_lon >= 3 and cols % 8 == 0
         and LANES % (cols * n_lon) == 0 and (rows // n_lon * cols * n_lon) % LANES == 0
         and args[2].shape[:2] == (7, 7) and channels % LANES == 0 and att % LANES == 0
-        and args[4].shape[1] == 3 * att
+        and args[4].shape[1] == 3 * att and 3 * att % ((STREAMS - 2) * LANES) == 0
     )
     return on_device(sizes, *args) if fits else on_device_native(*args)
 

time: 61.5 us -> 57.3 us (0.932)
  Pallas kernels: 60.6 us -> 56.5 us
    pallas_call x1, Pallas kernels: 57.7 us -> 53.5 us  [on_device(): pl.pallas_call(functools.partial(layer, sizes), out_shape=[shape((rows, c...]
where the time goes in v2:
time: 57.3 us; the launch traced here: 57.1 us
  Pallas kernels  56.5 us (99%)
  between operations  0.64 us (1%)
    pallas_call x1, Pallas kernels, on_device(): pl.pallas_call(functools.partial(layer, sizes), out_shape=[shape((rows, c...  53.5 us
    pallas_call x1, Pallas kernels, on_device(): pl.pallas_call(finish, out_shape=[shape((rows, cols, channels), bf16)] *...  2.95 us

profile of v2, /device:TPU:0, one launch (start us, length us, event | category | flops | bytes accessed | tf_op | source)
XLA Modules:
  0.0 57.1 jit_solution(18222768852340010085)
XLA Ops:
  0.6 53.5 %shard_map.109 = (bf16[32,8,512]{2,1,0:T(8,128)(2,1)}, bf16[32,8,512]{2,1,0:T(8,128)(2,1)}, bf16[4,64,512]{2,1,0:T(8,128)(2,1)}, bf16[4,16,512]{2,1,0:T(8,128)(2...) custom-call(bf16[32,8,512]{2,1,0:T(8,128)(2,1)} %bitcast.6, ...), custom_call_target="tpu_custom_call" | custom-call | tf_op jit(solution)/shard_map/pallas_call | solution.py:802
  54.2 3.0 %shard_map.110 = (bf16[32,8,512]{2,1,0:T(8,128)(2,1)}, bf16[32,8,512]{2,1,0:T(8,128)(2,1)}, f32[512,768]{1,0:T(8,128)}, f32[256,512]{1,0:T(8,128)}, f32[7,7,512]{2,1,0:T(8,128)}, /*index=5*/f32[1,512]{1,0:T(1,128)}) custom-call(bf16[32,8,512]{2,1,0:T(8,128)(2,1)} %get-tuple-element.22.refs_0_, bf16[32,8,512]{2,1,0:T(8,128)(2,1)} %get-tuple-element.23.refs_1_, ...), custom_call_target="tpu_custom_call" | custom-call | tf_op jit(solution)/shard_map/pallas_call | solution.py:820
